TPU v7x, 32 devices: a whole 2x2x4 slice. The times are simulated.
32 devices in a mesh: row: 4 (over x, core), col: 8 (over z, y).
Axes of the slice: x: 2, y: 2, z: 4, core: 2. Of those that a mesh axis runs over, the one named last changes fastest.
Arguments:
- amplitudes: bfloat16 [640, 90000], P(('row', 'col')), may hold values from -6 to 6
- coulomb: bfloat16 [90000, 8192], P('col', 'row'), may hold values from -0.01953125 to 0.01953125
Outputs:
- ladder: float32 [640, 8192], P('col', 'row')
All inputs are finite; a program needn't handle non-finite values.
Results may differ from a plain program's by a relative error of at most 0.0003.
Values may be sent and summed in bfloat16 or wider, within the bound.
A program may use at most 192 MiB of HBM per device.

v0:
```python
import jax
import jax.numpy as jnp
from jax import lax
from jax.sharding import PartitionSpec as P


def shards(amplitudes, coulomb):
    columns = lax.axis_size("col")
    grid_rows = lax.axis_size("row")
    pairs_here = amplitudes.shape[0]
    gathered = lax.all_gather(amplitudes, "row", axis=0, tiled=True)
    divided = lax.all_to_all(gathered, "col", split_axis=1, concat_axis=0, tiled=True)
    amp_panel = (
        divided.reshape(columns, grid_rows, pairs_here, -1)
        .transpose(1, 0, 2, 3)
        .reshape(columns * grid_rows * pairs_here, -1)
    )
    contraction = lax.psum_scatter(
        jnp.dot(amp_panel, coulomb, preferred_element_type=jnp.float32),
        "col",
        scatter_dimension=0,
        tiled=True,
    )
    return 0.5 * contraction


def solution(mesh):
    return jax.shard_map(
        shards,
        mesh=mesh,
        in_specs=(P(("row", "col"), None), P("col", "row")),
        out_specs=P("col", "row"),
        check_vma=False,
    )
```

profile of v0, /device:TPU:0, one launch (start us, length us, event | category | flops | bytes accessed | tf_op | source)
XLA Modules:
  0.0 709.9 jit_solution(15192235803599281325)
XLA Ops:
  6.5 0.0 all-gather.3.cloned.1.call-start
  6.5 0.7 all-gather.3.cloned.1.call-update
  7.3 0.0 reduce-scatter.2.cloned.1.call-start
  7.3 115.6 %all-gather.3.cloned.1.call-done = bf16[4,20,90000]{2,1,0:T(8,128)(2,1)} async-done(((bf16[1,20,90000]{2,1,0:T(8,128)(2,1)}), bf16[4,20,90000]{2,1,0:T(8,128)(2,1)}) %all-gather.3.cloned.1.call-update) | async-done | bytes 14400016 | tf_op jit(solution)/shard_map/all_gather | solution.py:11
  122.9 39.6 %all_to_all.12 = bf16[80,8,11250]{2,1,0:T(8,128)(2,1)} reshape(bf16[4,20,90000]{2,1,0:T(8,128)(2,1)} %all-gather.3.cloned.1.call-done) | data formatting | bytes 28800000 | tf_op jit(solution)/shard_map/all_to_all | solution.py:12
  162.6 9.2 %copy.6 = bf16[80,8,11250]{2,0,1:T(8,128)(2,1)S(1)} copy(bf16[80,8,11250]{2,1,0:T(8,128)(2,1)} %all_to_all.12) | data formatting | bytes 28800000 | tf_op jit(solution)/shard_map/all_to_all | solution.py:12
  171.8 318.0 %all_to_all.16 = bf16[80,8,11250]{2,0,1:T(8,128)(2,1)S(1)} all-to-all(bf16[80,8,11250]{2,0,1:T(8,128)(2,1)S(1)} %copy.6), channel_id=1, replica_groups=mesh['row'=4,'col'=8] {'col'}, dimensions={1} | all-to-all | bytes 28800000 | tf_op jit(solution)/shard_map/all_to_all | solution.py:12
  489.8 29.1 %copy.7 = bf16[80,8,11250]{2,1,0:T(8,128)(2,1)S(1)} copy(bf16[80,8,11250]{2,0,1:T(8,128)(2,1)S(1)} %all_to_all.16) | data formatting | bytes 28800000 | tf_op jit(solution)/shard_map/all_to_all | solution.py:12
  518.8 23.8 %copy.8 = bf16[4,8,20,11250]{3,2,1,0:T(8,128)(2,1)} copy(bf16[4,8,20,11250]{3,1,2,0:T(8,128)(2,1)S(1)} %bitcast.8) | data formatting | bytes 28800000 | tf_op jit(solution)/shard_map/transpose | solution.py:15
  542.7 19.0 %reshape.11 = bf16[640,11250]{1,0:T(8,128)(2,1)} reshape(bf16[4,8,20,11250]{3,2,1,0:T(8,128)(2,1)} %copy.8) | data formatting | bytes 28800000 | tf_op jit(solution)/shard_map/reshape | solution.py:16
  561.7 38.1 %fusion = f32[640,2048]{1,0:T(8,128)} fusion(bf16[640,11250]{1,0:T(8,128)(2,1)} %reshape.11, bf16[11250,2048]{1,0:T(8,128)(2,1)} %param.3), kind=kOutput, calls=%fused_computation.1 | convolution fusion | flops 29491200000 | bytes 65722880 | tf_op jit(solution)/shard_map/dot_general | solution.py:19
  599.8 0.0 reduce-scatter.2.cloned.1.call-update
  599.8 101.3 %reduce-scatter.2.cloned.1.call-done = f32[80,2048]{1,0:T(8,128)} async-done(((f32[640,2048]{1,0:T(8,128)}), f32[80,2048]{1,0:T(8,128)}) %reduce-scatter.2.cloned.1.call-update) | async-done | bytes 655376 | tf_op jit(solution)/shard_map/reduce_scatter | solution.py:18
  701.1 2.0 broadcast_multiply_fusion
Async XLA Ops:
  6.5 116.4 %all-gather.3.cloned.1.call-start = ((), (), s32[]{:S(2)}) async-start(), calls=%async_computation.3 | async-start | bytes 21626880 | tf_op jit(solution)/shard_map/all_gather | solution.py:11
  7.3 693.8 %reduce-scatter.2.cloned.1.call-start = ((), (), s32[]{:S(2)}) async-start(), calls=%async_computation.2 | async-start | bytes 5898240 | tf_op jit(solution)/shard_map/reduce_scatter | solution.py:18
Sparse Core Ops, SparseCore 0:
  8.9 113.9 all-gather.2
  599.9 101.1 reduce-scatter.1
where the time goes:
time: 711 us; the launch traced here: 710 us
  blocking collectives  318 us (45%)
  waiting for transfers between devices  218 us (31%)
  local copies, waits for them, and re-layouts  121 us (17%)
  matrix products  38.1 us (5%)
  between operations  13.4 us (2%)
    all_to_all x1, blocking collectives, shards(): lax.all_to_all(gathered, 'col', split_axis=1, concat_axis=0, tiled=True)  318 us
    all_gather x1, waiting for transfers between devices, shards(): gathered = lax.all_gather(amplitudes, 'row', axis=0, tiled=True)  116 us
    reduce_scatter x1, waiting for transfers between devices, shards(): lax.psum_scatter(jnp.dot(amp_panel, coulomb, preferred_element_type=jnp.f...  101 us
    all_to_all x3, local copies, waits for them, and re-layouts, shards(): lax.all_to_all(gathered, 'col', split_axis=1, concat_axis=0, tiled=True)  77.9 us
    dot_general x1, matrix products, shards(): jnp.dot(amp_panel, coulomb, preferred_element_type=jnp.float32)  38.1 us
    transpose x1, local copies, waits for them, and re-layouts, shards(): amp_panel = divided.reshape(columns, grid_rows, pairs_here, -1).transpose...  23.8 us
    reshape x1, local copies, waits for them, and re-layouts, shards(): amp_panel = divided.reshape(columns, grid_rows, pairs_here, -1).transpose...  19 us
  transfers between devices with their start and end apart: 2, of which 2 were waited for; matrix products, arithmetic and copies ran while one was open for 0% of the time, Pallas kernels for 0%

commit v1 on v0

--- a/solution.py
+++ b/solution.py
@@ -4,11 +4,32 @@
 from jax.sharding import PartitionSpec as P
 
 
+def in_order(pieces, dim):
+    pieces = jnp.moveaxis(pieces, 0, dim)
+    dims = pieces.shape
+    return pieces.reshape(*dims[:dim], dims[dim] * dims[dim + 1], *dims[dim + 2 :])
+
+
+def grow_blocks(array, axis):
+    length, index = (lax.axis_size(axis), lax.axis_index(axis))
+    blocks, distance = (array[None], 1)
+    while distance < length:
+        other = lax.ppermute(blocks, axis, [(i, i ^ distance) for i in range(length)])
+        low = index & distance == 0
+        blocks = jnp.concatenate([jnp.where(low, blocks, other), jnp.where(low, other, blocks)])
+        distance *= 2
+    return blocks
+
+
+def doubled_up(value, axis, dim):
+    return in_order(grow_blocks(value, axis), dim)
+
+
 def shards(amplitudes, coulomb):
     columns = lax.axis_size("col")
     grid_rows = lax.axis_size("row")
     pairs_here = amplitudes.shape[0]
-    gathered = lax.all_gather(amplitudes, "row", axis=0, tiled=True)
+    gathered = doubled_up(amplitudes, "row", 0)
     divided = lax.all_to_all(gathered, "col", split_axis=1, concat_axis=0, tiled=True)
     amp_panel = (
         divided.reshape(columns, grid_rows, pairs_here, -1)

time: 711 us -> 809 us (1.14)
  waiting for transfers between devices: 218 us -> 265 us
  other arithmetic: 1.97 us -> 38.1 us
  local copies, waits for them, and re-layouts: 121 us -> 133 us
    ppermute x0 -> x2, waiting for transfers between devices: none -> 163 us  [grow_blocks(): lax.ppermute(blocks, axis, [(i, i ^ distance) for i in range(length)])]
    all_gather x1 -> x0, waiting for transfers between devices: 116 us -> none  [shards(): gathered = lax.all_gather(amplitudes, 'row', axis=0, tiled=True)]
    select_n x0 -> x2, other arithmetic: none -> 18.6 us  [grow_blocks(): jnp.where(low, blocks, other)]
    concatenate x0 -> x2, other arithmetic: none -> 17.5 us  [grow_blocks(): jnp.concatenate([jnp.where(low, blocks, other), jnp.where(low, other, blo...]
    concatenate x0 -> x1, local copies, waits for them, and re-layouts: none -> 11.8 us  [grow_blocks(): jnp.concatenate([jnp.where(low, blocks, other), jnp.where(low, other, blo...]
  transfers between devices with their start and end apart: 2 -> 3, of which waited for: 2 -> 3; matrix products, arithmetic and copies ran while one was open for 0% -> 0% of each run, Pallas kernels for 0% -> 0%
where the time goes in v1:
time: 809 us; the launch traced here: 808 us
  blocking collectives  318 us (39%)
  waiting for transfers between devices  265 us (33%)
  local copies, waits for them, and re-layouts  133 us (16%)
  other arithmetic  38.1 us (5%)
  matrix products  38.1 us (5%)
  between operations  13.4 us (2%)
    all_to_all x1, blocking collectives, shards(): lax.all_to_all(gathered, 'col', split_axis=1, concat_axis=0, tiled=True)  318 us
    ppermute x2, waiting for transfers between devices, grow_blocks(): lax.ppermute(blocks, axis, [(i, i ^ distance) for i in range(length)])  163 us
    reduce_scatter x1, waiting for transfers between devices, shards(): lax.psum_scatter(jnp.dot(amp_panel, coulomb, preferred_element_type=jnp.f...  101 us
    all_to_all x3, local copies, waits for them, and re-layouts, shards(): lax.all_to_all(gathered, 'col', split_axis=1, concat_axis=0, tiled=True)  77.9 us
    dot_general x1, matrix products, shards(): jnp.dot(amp_panel, coulomb, preferred_element_type=jnp.float32)  38.1 us
    transpose x1, local copies, waits for them, and re-layouts, shards(): amp_panel = divided.reshape(columns, grid_rows, pairs_here, -1).transpose...  23.8 us
    reshape x1, local copies, waits for them, and re-layouts, shards(): amp_panel = divided.reshape(columns, grid_rows, pairs_here, -1).transpose...  19 us
    select_n x2, other arithmetic, grow_blocks(): jnp.where(low, blocks, other)  18.6 us
  transfers between devices with their start and end apart: 3, of which 3 were waited for; matrix products, arithmetic and copies ran while one was open for 0% of the time, Pallas kernels for 0%

profile of v1, /device:TPU:0, one launch (start us, length us, event | category | flops | bytes accessed | tf_op | source)
XLA Modules:
  0.0 808.3 jit_solution(11204823487345116395)
XLA Ops:
  6.5 0.0 reduce-scatter.2.cloned.1.call-start
  6.5 0.5 collective-permute-start
  7.0 7.3 collective-permute-done
  14.3 6.1 broadcast_select_fusion.3
  20.4 0.0 copy-start
  20.5 8.3 %pad_maximum_fusion.1 = bf16[2,20,90000]{2,1,0:T(8,128)(2,1)} fusion(bf16[1,20,90000]{2,1,0:T(8,128)(2,1)} %get-tuple-element.8, bf16[1,20,90000]{2,1,0:T(8,128)(2,1)S(1)} %get-tuple-element.7), kind=kLoop, calls=%fused_computation.1 | loop fusion | flops 3600000 | bytes 14400000 | tf_op jit(solution)/shard_map/concatenate | solution.py:19
  28.7 0.0 copy-done
  28.7 11.8 %copy.7 = bf16[2,20,90000]{2,0,1:T(2,128)(2,1)} copy(bf16[2,20,90000]{2,1,0:T(8,128)(2,1)} %pad_maximum_fusion.1) | data formatting | bytes 14400000 | tf_op jit(solution)/shard_map/concatenate | solution.py:19
  40.5 2.8 collective-permute-start.1
  43.4 155.8 %collective-permute-done.1 = bf16[2,20,90000]{2,0,1:T(2,128)(2,1)} collective-permute-done((bf16[2,20,90000]{2,0,1:T(2,128)(2,1)}, bf16[2,20,90000]{2,0,1:T(2,128)(2,1)}, u32[]{:S(2)}, u32[]{:S(2)}) %collective-permute-start.1) | collective-permute-done | bytes 7200032 | tf_op jit(solution)/shard_map/ppermute | solution.py:17
  199.2 12.5 %broadcast_select_fusion.1 = (bf16[2,20,90000]{2,1,0:T(8,128)(2,1)S(1)}, bf16[2,20,90000]{2,1,0:T(8,128)(2,1)S(1)}) fusion(pred[]{:T(512)S(6)} %eq.6, bf16[2,20,90000]{2,0,1:T(2,128)(2,1)} %collective-permute-done.1, bf16[1,20,90000]{2,1,0:T(8,128)(2,1)} %get-tuple-element.8, bf16[1,20,90000]{2,1,0:T(8,128)(2,1)} %copy-done), kind=kLoop, calls=%fused_computation.3 | loop fusion | flops 10800000 | bytes 28800000 | tf_op jit(solution)/shard_map/jit(_where)/select_n | solution.py:19
  211.6 9.2 %pad_maximum_fusion = bf16[4,20,90000]{2,1,0:T(8,128)(2,1)} fusion(bf16[2,20,90000]{2,1,0:T(8,128)(2,1)S(1)} %get-tuple-element.6, bf16[2,20,90000]{2,1,0:T(8,128)(2,1)S(1)} %get-tuple-element.5), kind=kLoop, calls=%fused_computation | loop fusion | flops 7200000 | bytes 28800000 | tf_op jit(solution)/shard_map/concatenate | solution.py:19
  220.9 39.7 %all_to_all.12 = bf16[80,8,11250]{2,1,0:T(8,128)(2,1)} reshape(bf16[4,20,90000]{2,1,0:T(8,128)(2,1)} %pad_maximum_fusion) | data formatting | bytes 28800000 | tf_op jit(solution)/shard_map/all_to_all | solution.py:33
  260.5 9.2 %copy.10 = bf16[80,8,11250]{2,0,1:T(8,128)(2,1)S(1)} copy(bf16[80,8,11250]{2,1,0:T(8,128)(2,1)} %all_to_all.12) | data formatting | bytes 28800000 | tf_op jit(solution)/shard_map/all_to_all | solution.py:33
  269.7 318.3 %all_to_all.16 = bf16[80,8,11250]{2,0,1:T(8,128)(2,1)S(1)} all-to-all(bf16[80,8,11250]{2,0,1:T(8,128)(2,1)S(1)} %copy.10), channel_id=1, replica_groups=mesh['row'=4,'col'=8] {'col'}, dimensions={1} | all-to-all | bytes 28800000 | tf_op jit(solution)/shard_map/all_to_all | solution.py:33
  588.0 29.1 %copy.11 = bf16[80,8,11250]{2,1,0:T(8,128)(2,1)S(1)} copy(bf16[80,8,11250]{2,0,1:T(8,128)(2,1)S(1)} %all_to_all.16) | data formatting | bytes 28800000 | tf_op jit(solution)/shard_map/all_to_all | solution.py:33
  617.1 23.8 %copy.12 = bf16[4,8,20,11250]{3,2,1,0:T(8,128)(2,1)} copy(bf16[4,8,20,11250]{3,1,2,0:T(8,128)(2,1)S(1)} %bitcast.10) | data formatting | bytes 28800000 | tf_op jit(solution)/shard_map/transpose | solution.py:36
  640.9 19.0 %reshape.13 = bf16[640,11250]{1,0:T(8,128)(2,1)} reshape(bf16[4,8,20,11250]{3,2,1,0:T(8,128)(2,1)} %copy.12) | data formatting | bytes 28800000 | tf_op jit(solution)/shard_map/reshape | solution.py:37
  659.9 38.1 %fusion = f32[640,2048]{1,0:T(8,128)} fusion(bf16[640,11250]{1,0:T(8,128)(2,1)} %reshape.13, bf16[11250,2048]{1,0:T(8,128)(2,1)} %param.3), kind=kOutput, calls=%fused_computation.7 | convolution fusion | flops 29491200000 | bytes 65722880 | tf_op jit(solution)/shard_map/dot_general | solution.py:40
  698.0 0.0 reduce-scatter.2.cloned.1.call-update
  698.1 101.4 %reduce-scatter.2.cloned.1.call-done = f32[80,2048]{1,0:T(8,128)} async-done(((f32[640,2048]{1,0:T(8,128)}), f32[80,2048]{1,0:T(8,128)}) %reduce-scatter.2.cloned.1.call-update) | async-done | bytes 655376 | tf_op jit(solution)/shard_map/reduce_scatter | solution.py:39
  799.5 2.0 broadcast_multiply_fusion
Async XLA Ops:
  6.5 793.0 %reduce-scatter.2.cloned.1.call-start = ((), (), s32[]{:S(2)}) async-start(), calls=%async_computation.2 | async-start | bytes 5898240 | tf_op jit(solution)/shard_map/reduce_scatter | solution.py:39
  6.5 7.8 collective-permute-start
  20.4 8.3 %copy-start = (bf16[1,20,90000]{2,1,0:T(8,128)(2,1)}, bf16[1,20,90000]{2,1,0:T(8,128)(2,1)S(1)}, u32[]{:S(2)}) copy-start(bf16[1,20,90000]{2,1,0:T(8,128)(2,1)S(1)} %get-tuple-element.7) | copy-start | bytes 10800004
  40.5 158.6 %collective-permute-start.1 = (bf16[2,20,90000]{2,0,1:T(2,128)(2,1)}, bf16[2,20,90000]{2,0,1:T(2,128)(2,1)}, u32[]{:S(2)}, u32[]{:S(2)}) collective-permute-start(bf16[2,20,90000]{2,0,1:T(2,128)(2,1)} %copy.7), channel_id=1, source_target_pairs={{0,16},{8,24},{16,0},{24,8},{1,17},{9,25},{17,1},{25,9},{2,18},{10... | collective-permute-start | bytes 21600008 | tf_op jit(solution)/shard_map/ppermute | solution.py:17
Sparse Core Ops, SparseCore 0:
  698.2 101.2 reduce-scatter.1
